TPU v7x, 512 devices: a whole 4x8x8 slice. The times are simulated.
512 devices in a mesh: seq: 64 (over z, y_hi, core), head: 8 (over x, y_lo).
Axes of the slice: x: 4, y: 8 (y_hi: 4, y_lo: 2; y = y_hi * 2 + y_lo), z: 8, core: 2. Of those that a mesh axis runs over, the one named last changes fastest.
Arguments:
- block_query_rows: bfloat16 [8192, 5120], P('seq', 'head'), may hold values from -180 to 180
- block_key_rows: bfloat16 [8192, 1024], P('seq', 'head'), may hold values from -6 to 6
- block_value_rows: bfloat16 [8192, 1024], P('seq', 'head'), may hold values from -6 to 6
- stretch_segments: int32 [8192], P('seq'), may hold values from 0 to 15, never falling along the last dimension, each value on 1 to 6144 neighbouring positions
- residual: bfloat16 [8192, 5120], P('seq', 'head'), may hold values from -6 to 6
- out_weight: bfloat16 [5120, 5120], P('head', 'seq'), may hold values from -0.25 to 0.25
- cache_by_prefill: bfloat16 [2, 2, 2048, 16, 1024], P(None, None, 'seq', None, 'head'), may hold values from -6 to 6
- request_pages: int32 [128], replicated, may hold values from 1 to 64, as said below
- request_owner: int32 [128], replicated, may hold values from 0 to 63, as said below
Outputs:
- layer_out: bfloat16 [8192, 5120], P('seq', 'head')
- cache_decode: bfloat16 [2, 2, 4096, 16, 1024], P(None, None, 'seq', None, 'head')
Inputs may be any that keep to these rules, and one draw needn't show every extreme that they name: `stretch_segments`: each request of the block holds at most 6144 tokens, and some request exactly that many. `request_pages`: the requests of one decode device hold at most 64 pages together, and those of some device exactly 64. `request_owner`: never falls along the requests; every device owns at least one request.
All inputs are finite; a program needn't handle non-finite values.
Results may differ from a plain program's by a relative error of at most 0.0065.
Values may be sent and summed in bfloat16 or wider, within the bound.
A program may use at most 128 MiB of HBM per device.

v0:
```python
import jax
import jax.numpy as jnp
from jax import lax
from jax.sharding import PartitionSpec as P

HEAD_SIZE = 128


def on_device(
    block_query_rows,
    block_key_rows,
    block_value_rows,
    stretch_segments,
    residual,
    out_weight,
    cache_by_prefill,
    request_pages,
    request_owner,
):
    seq_count = lax.axis_size("seq")
    seq_place = lax.axis_index("seq")
    rows = block_query_rows.shape[0]
    kv_local = block_key_rows.shape[1] // HEAD_SIZE
    query_groups = block_query_rows.shape[1] // block_key_rows.shape[1]
    query_four = block_query_rows.reshape(rows, kv_local, query_groups, HEAD_SIZE)
    query_place = seq_place * rows + jnp.arange(rows, dtype=jnp.int32)
    scale = HEAD_SIZE ** (-0.5)
    key_part = lax.all_gather(block_key_rows, "seq", axis=0, tiled=True)
    value_part = lax.all_gather(block_value_rows, "seq", axis=0, tiled=True)
    segment_part = lax.all_gather(stretch_segments, "seq", axis=0, tiled=True)
    count = key_part.shape[0]
    key_place = jnp.arange(count, dtype=jnp.int32)
    allowed = (
        (stretch_segments[:, None] == segment_part[None, :])
        & (query_place[:, None] >= key_place[None, :])
        & (key_place[None, :] >= 0)
    )
    running_max = jnp.full((kv_local, query_groups, rows), -1e30, jnp.float32)
    key_three = key_part.reshape(count, kv_local, HEAD_SIZE)
    value_three = value_part.reshape(count, kv_local, HEAD_SIZE)
    scores = (
        jnp.einsum("tkgd,pkd->kgtp", query_four, key_three, preferred_element_type=jnp.float32)
        * scale
    )
    masked = jnp.where(allowed, scores, -1e30)
    new_max = jnp.maximum(running_max, jnp.max(masked, axis=-1))
    weights = jnp.where(allowed, jnp.exp(masked - new_max[..., None]), 0.0)
    new_sum = jnp.sum(weights, axis=-1)
    contribution = jnp.einsum(
        "kgtp,pkd->kgtd",
        weights.astype(jnp.bfloat16),
        value_three,
        preferred_element_type=jnp.float32,
    )
    attention = (
        jnp.transpose(contribution / new_sum[..., None], (2, 0, 1, 3))
        .reshape(rows, -1)
        .astype(jnp.bfloat16)
    )
    partial_value = jnp.dot(
        attention,
        lax.all_gather(out_weight, "seq", axis=1, tiled=True),
        preferred_element_type=jnp.float32,
    )
    feature_width = partial_value.shape[1] // lax.axis_size("head")
    total = lax.psum(partial_value.astype(jnp.bfloat16), "head").astype(jnp.float32)
    mine = lax.dynamic_slice_in_dim(total, lax.axis_index("head") * feature_width, feature_width, 1)
    layer_out = (residual.astype(jnp.float32) + mine).astype(jnp.bfloat16)
    local_pages = cache_by_prefill.shape[2]
    capacity = 2 * local_pages
    per_pair = capacity // seq_count
    owners = jnp.arange(seq_count, dtype=jnp.int32)
    run_pages = jnp.sum(
        jnp.where(request_owner[None, :] == owners[:, None], request_pages[None, :], 0), axis=1
    )
    run_start = jnp.sum(
        jnp.where(request_owner[None, :] < owners[:, None], request_pages[None, :], 0), axis=1
    )
    pair_slots = jnp.arange(per_pair, dtype=jnp.int32)
    offset = (seq_place - run_start) % seq_count
    slot_index = pair_slots[None, :] * seq_count + offset[:, None]
    sending = slot_index < run_pages[:, None]
    local_index = pair_slots[None, :] + ((run_start + offset - seq_place) // seq_count)[:, None]
    local_index = jnp.where(sending, local_index, 0).reshape(-1)
    picked = jnp.take(cache_by_prefill, local_index, axis=2)
    outgoing = jnp.where(
        sending.reshape(-1)[None, None, :, None, None], picked, jnp.zeros_like(picked)
    )
    incoming = lax.all_to_all(outgoing, "seq", split_axis=2, concat_axis=2, tiled=True)
    layers, pair_kv, _, page_len, width = incoming.shape
    arranged = jnp.swapaxes(
        incoming.reshape(layers, pair_kv, seq_count, per_pair, page_len, width), 2, 3
    )
    my_start = run_start[seq_place]
    my_pages = run_pages[seq_place]
    rotated = jnp.roll(arranged, -my_start, axis=3).reshape(
        layers, pair_kv, capacity, page_len, width
    )
    keep = jnp.arange(capacity, dtype=jnp.int32) < my_pages
    cache_decode = jnp.where(keep[None, None, :, None, None], rotated, jnp.zeros_like(rotated))
    return (layer_out, cache_decode)


def solution(mesh):
    return jax.shard_map(
        on_device,
        mesh=mesh,
        in_specs=(
            P("seq", "head"),
            P("seq", "head"),
            P("seq", "head"),
            P("seq"),
            P("seq", "head"),
            P("head", "seq"),
            P(None, None, "seq", None, "head"),
            P(),
            P(),
        ),
        out_specs=(P("seq", "head"), P(None, None, "seq", None, "head")),
        check_vma=False,
    )
```

profile of v0, /device:TPU:16, one launch (start us, length us, event | category | flops | bytes accessed | tf_op | source)
XLA Modules:
  0.0 391.2 jit_solution(16656007094815539979)
XLA Ops:
  7.2 0.0 copy-start
  7.2 0.0 all-gather.5.cloned.1.call-start
  7.2 0.7 all-gather.5.cloned.1.call-update
  7.9 0.0 all-gather.7.cloned.1.call-start
  8.0 1.5 copy.27
  9.4 0.0 all-gather.7.cloned.1.call-update
  9.5 0.0 all-gather.9.cloned.1.call-start
  9.5 0.7 all-gather.9.cloned.1.call-update
  10.2 0.8 select_reduce_fusion.1
  11.0 0.0 copy-done
  11.0 0.8 gather_fusion
  11.9 1.2 select_bitcast_fusion
  13.1 16.5 %all-to-all-start = ((bf16[2,2,64,16,128]{4,3,1,0,2:T(8,128)(2,1)}), bf16[2,2,64,16,128]{4,3,1,0,2:T(8,128)(2,1)S(1)}, u32[]{:S(2)}, u32[]{:S(2)}) async-start(bf16[2,2,64,16,128]{4,3,1,0,2:T(8,128)(2,1)} %select_bitcast_fusion), calls=%async_computation | async-start | bytes 2097152 | tf_op jit(solution)/shard_map/all_to_all | solution.py:89
  29.5 0.0 all-reduce.2.cloned.1.call-start
  29.6 1.1 copy.25
  30.7 98.7 %all-gather = s32[64,1,128]{2,1,0:T(1,128)S(1)} all-gather(s32[1,1,128]{2,1,0:T(1,128)} %bitcast.79), channel_id=1, replica_groups=mesh['seq'=64,'head'=8] {'seq'}, dimensions={0}, use_global_device_ids=true | all-gather | bytes 33280 | tf_op jit(solution)/shard_map/all_gather | solution.py:30
  129.4 4.4 %fusion.7 = pred[128,8192]{0,1:T(8,128)(4,1)S(1)} fusion(s32[128]{0:T(128)S(1)} %iota_add_fusion, s32[128]{0:T(128)} %param.12, s32[8192]{0:T(1024)S(1)} %bitcast.78), kind=kLoop, calls=%fused_computation.11 | loop fusion | flops 3145728 | bytes 1082368 | tf_op jit(solution)/shard_map/and | solution.py:34
  133.8 0.0 all-gather.5.cloned.1.call-done
  133.8 4.7 %fusion = (f32[5,128]{1,0:T(8,128)S(1)}, f32[8192,128,5]{1,0,2:T(8,128)S(1)}) fusion(pred[128,8192]{0,1:T(8,128)(4,1)S(1)} %fusion.7, bf16[128,5,128]{0,2,1:T(8,128)(2,1)S(1)} %bitcast.76, bf16[8192,128]{1,0:T(8,128)(2,1)} %all-gather.5.cloned.1.call-done), kind=kOutput, calls=%fused_computation.3 | convolution fusion | flops 1357905280 | bytes 24283648 | tf_op jit(solution)/shard_map/tkgd,pkd->kgtp/dot_general | solution.py:42
  138.6 0.0 copy-start.1
  138.6 6.9 %copy-done.1 = f32[8192,128,5]{1,0,2:T(8,128)} copy-done((f32[8192,128,5]{1,0,2:T(8,128)}, f32[8192,128,5]{1,0,2:T(8,128)S(1)}, u32[]{:S(2)}) %copy-start.1) | copy-done | bytes 20971544
  145.5 5.2 %fusion.1 = f32[5,128]{1,0:T(8,128)S(1)} fusion(f32[8192,128,5]{1,0,2:T(8,128)S(1)} %get-tuple-element.7, f32[5,128]{1,0:T(8,128)S(1)} %broadcast_maximum_fusion, pred[128,8192]{0,1:T(8,128)(4,1)S(1)} %fusion.7), kind=kLoop, calls=%fused_computation.4 | loop fusion | flops 26213760 | bytes 22025216 | tf_op jit(solution)/shard_map/reduce_sum | solution.py:48
  150.7 40.7 %all-gather.7.cloned.1.call-done = bf16[8192,128]{0,1:T(8,128)(2,1)} async-done(((bf16[128,128]{0,1:T(8,128)(2,1)}), bf16[8192,128]{0,1:T(8,128)(2,1)}) %all-gather.7.cloned.1.call-update) | async-done | bytes 2097168 | tf_op jit(solution)/shard_map/all_gather | solution.py:29
  191.4 12.9 %fusion.16 = bf16[5,128,128]{1,2,0:T(8,128)(2,1)S(1)} fusion(f32[8192,128,5]{1,0,2:T(8,128)} %copy-done.1, f32[5,128]{1,0:T(8,128)S(1)} %broadcast_maximum_fusion, pred[128,8192]{0,1:T(8,128)(4,1)S(1)} %fusion.7, bf16[8192,128]{0,1:T(8,128)(2,1)} %all-gather.7.cloned.1.call-done, f32[5,128]{1,0:T(8,128)S(1)} %fusion.1), kind=kOutput, calls=%fused_computation.18 | convolution fusion | flops 1368555520 | bytes 24286208 | tf_op jit(solution)/shard_map/kgtp,pkd->kgtd/dot_general | solution.py:49
  204.3 0.0 copy-start.2
  204.4 81.0 %all-gather.9.cloned.1.call-done = bf16[640,5120]{0,1:T(8,128)(2,1)} async-done(((bf16[640,80]{0,1:T(8,128)(2,1)}), bf16[640,5120]{0,1:T(8,128)(2,1)}) %all-gather.9.cloned.1.call-update) | async-done | bytes 6553616 | tf_op jit(solution)/shard_map/all_gather | solution.py:62
  285.3 6.2 %convolution_convert_fusion = bf16[128,5120]{1,0:T(8,128)(2,1)} fusion(bf16[128,640]{0,1:T(8,128)(2,1)S(1)} %bitcast.77, bf16[640,5120]{0,1:T(8,128)(2,1)} %all-gather.9.cloned.1.call-done), kind=kOutput, calls=%fused_computation.9 | convolution fusion | flops 839516160 | bytes 8028160 | tf_op jit(solution)/shard_map/dot_general | solution.py:60
  291.5 0.0 all-reduce.2.cloned.1.call-update
  291.5 0.6 dynamic_slice.14
  292.1 0.6 dynamic_slice.15
  294.1 0.7 iota_compare_fusion.3
  294.7 0.0 all-to-all-done
  294.7 1.5 bitcast_select_fusion.1
  296.2 86.8 %all-reduce.2.cloned.1.call-done = bf16[128,5120]{1,0:T(8,128)(2,1)} async-done(((bf16[128,5120]{1,0:T(8,128)(2,1)}), bf16[128,5120]{1,0:T(8,128)(2,1)}) %all-reduce.2.cloned.1.call-update) | async-done | bytes 1310736 | tf_op jit(solution)/shard_map/psum | solution.py:66
  383.0 0.0 copy-done.2
  383.0 1.6 add_convert_fusion
  (5 shorter events, 0.1 us)
Async XLA Ops:
  7.2 3.9 copy-start
  7.2 126.6 %all-gather.5.cloned.1.call-start = ((), (), s32[]{:S(2)}) async-start(), calls=%async_computation.1 | async-start | bytes 2129920 | tf_op jit(solution)/shard_map/all_gather | solution.py:28
  7.9 183.5 %all-gather.7.cloned.1.call-start = ((), (), s32[]{:S(2)}) async-start(), calls=%async_computation.2 | async-start | bytes 2129920 | tf_op jit(solution)/shard_map/all_gather | solution.py:29
  9.5 275.9 %all-gather.9.cloned.1.call-start = ((), (), s32[]{:S(2)}) async-start(), calls=%async_computation.3 | async-start | bytes 6656000 | tf_op jit(solution)/shard_map/all_gather | solution.py:62
  13.1 281.6 %all-to-all-start = ((bf16[2,2,64,16,128]{4,3,1,0,2:T(8,128)(2,1)}), bf16[2,2,64,16,128]{4,3,1,0,2:T(8,128)(2,1)S(1)}, u32[]{:S(2)}, u32[]{:S(2)}) async-start(bf16[2,2,64,16,128]{4,3,1,0,2:T(8,128)(2,1)} %select_bitcast_fusion), calls=%async_computation | async-start | bytes 2097152 | tf_op jit(solution)/shard_map/all_to_all | solution.py:89
  29.5 353.5 %all-reduce.2.cloned.1.call-start = ((), (), s32[]{:S(2)}) async-start(), calls=%async_computation.4 | async-start | bytes 2621440 | tf_op jit(solution)/shard_map/psum | solution.py:66
  138.6 7.0 %copy-start.1 = (f32[8192,128,5]{1,0,2:T(8,128)}, f32[8192,128,5]{1,0,2:T(8,128)S(1)}, u32[]{:S(2)}) copy-start(f32[8192,128,5]{1,0,2:T(8,128)S(1)} %get-tuple-element.7) | copy-start | bytes 62914564
  204.3 178.7 %copy-start.2 = (bf16[128,640]{1,0:T(8,128)(2,1)S(1)}, bf16[128,640]{1,0:T(8,128)(2,1)}, u32[]{:S(2)}) copy-start(bf16[128,640]{1,0:T(8,128)(2,1)} %param.13) | copy-start | bytes 491524
Sparse Core Ops, SparseCore 0:
  11.3 100.3 all-gather.4
  115.5 75.8 all-gather.6
  194.7 90.5 all-gather.8
  291.6 91.3 all-reduce.1
where the time goes:
time: 392 us; the launch traced here: 391 us
  waiting for transfers between devices  210 us (54%)
  blocking collectives  98.7 us (25%)
  matrix products  23.8 us (6%)
  starting transfers between devices  16.6 us (4%)
  other arithmetic  15.4 us (4%)
  between operations  15.2 us (4%)
  local copies, waits for them, and re-layouts  11.5 us (3%)
    all_gather x1, blocking collectives, on_device(): segment_part = lax.all_gather(stretch_segments, 'seq', axis=0, tiled=True)  98.7 us
    psum x1, waiting for transfers between devices, on_device(): lax.psum(partial_value.astype(jnp.bfloat16), 'head').astype(jnp.float32)  86.8 us
    all_gather x1, waiting for transfers between devices, on_device(): lax.all_gather(out_weight, 'seq', axis=1, tiled=True)  81 us
    all_gather x1, waiting for transfers between devices, on_device(): value_part = lax.all_gather(block_value_rows, 'seq', axis=0, tiled=True)  40.7 us
    all_to_all x1, starting transfers between devices, on_device(): lax.all_to_all(outgoing, 'seq', split_axis=2, concat_axis=2, tiled=True)  16.5 us
    dot_general x1, matrix products, on_device(): jnp.einsum('kgtp,pkd->kgtd', weights.astype(jnp.bfloat16), value_three, p...  12.9 us
    unnamed x8, local copies, waits for them, and re-layouts  9.51 us
  transfers between devices with their start and end apart: 5, of which 3 were waited for; matrix products, arithmetic and copies ran while one was open for 11% of the time, Pallas kernels for 0%

commit v1 on v0

--- a/solution.py
+++ b/solution.py
@@ -26,7 +26,9 @@
     query_place = seq_place * rows + jnp.arange(rows, dtype=jnp.int32)
     scale = HEAD_SIZE ** (-0.5)
     key_part = lax.all_gather(block_key_rows, "seq", axis=0, tiled=True)
-    value_part = lax.all_gather(block_value_rows, "seq", axis=0, tiled=True)
+    value_part = jnp.concatenate(
+        lax.all_to_all(jnp.stack([block_value_rows] * lax.axis_size("seq")), "seq", 0, 0), axis=0
+    )
     segment_part = lax.all_gather(stretch_segments, "seq", axis=0, tiled=True)
     count = key_part.shape[0]
     key_place = jnp.arange(count, dtype=jnp.int32)

time: 392 us -> 360 us (0.918)
  waiting for transfers between devices: 210 us -> 129 us
  blocking collectives: 98.7 us -> 125 us
  starting transfers between devices: 16.6 us -> 32.1 us
  local copies, waits for them, and re-layouts: 11.5 us -> 19.1 us
    all_gather x1 -> x0, waiting for transfers between devices: 40.7 us -> none  [on_device(): value_part = lax.all_gather(block_value_rows, 'seq', axis=0, tiled=True)]
    all_gather x1, waiting for transfers between devices: 81 us -> 42.3 us  [on_device(): lax.all_gather(out_weight, 'seq', axis=1, tiled=True)]
    all_gather x1, blocking collectives: 98.7 us -> 125 us  [on_device(): segment_part = lax.all_gather(stretch_segments, 'seq', axis=0, tiled=True)]
    all_to_all x0 -> x1, starting transfers between devices: none -> 16.5 us  [on_device(): lax.all_to_all(jnp.stack([block_value_rows] * lax.axis_size('seq')), 'seq...]
    another operation x0 -> x2, local copies, waits for them, and re-layouts: none -> 4.65 us
    unnamed x8 -> x12, local copies, waits for them, and re-layouts: 9.51 us -> 8.91 us
  transfers between devices with their start and end apart: 5 -> 5, of which waited for: 3 -> 2; matrix products, arithmetic and copies ran while one was open for 11% -> 14% of each run, Pallas kernels for 0% -> 0%
where the time goes in v1:
time: 360 us; the launch traced here: 359 us
  waiting for transfers between devices  129 us (36%)
  blocking collectives  125 us (35%)
  starting transfers between devices  32.1 us (9%)
  matrix products  20.9 us (6%)
  local copies, waits for them, and re-layouts  19.1 us (5%)
  other arithmetic  17.8 us (5%)
  between operations  15.2 us (4%)
    all_gather x1, blocking collectives, on_device(): segment_part = lax.all_gather(stretch_segments, 'seq', axis=0, tiled=True)  125 us
    psum x1, waiting for transfers between devices, on_device(): lax.psum(partial_value.astype(jnp.bfloat16), 'head').astype(jnp.float32)  85.6 us
    all_gather x1, waiting for transfers between devices, on_device(): lax.all_gather(out_weight, 'seq', axis=1, tiled=True)  42.3 us
    all_to_all x1, starting transfers between devices, on_device(): lax.all_to_all(jnp.stack([block_value_rows] * lax.axis_size('seq')), 'seq...  16.5 us
    all_to_all x1, starting transfers between devices, on_device(): lax.all_to_all(outgoing, 'seq', split_axis=2, concat_axis=2, tiled=True)  15.3 us
    dot_general x1, matrix products, on_device(): jnp.einsum('kgtp,pkd->kgtd', weights.astype(jnp.bfloat16), value_three, p...  9.71 us
    unnamed x12, local copies, waits for them, and re-layouts  8.91 us
  transfers between devices with their start and end apart: 5, of which 2 were waited for; matrix products, arithmetic and copies ran while one was open for 14% of the time, Pallas kernels for 0%

profile of v1, /device:TPU:16, one launch (start us, length us, event | category | flops | bytes accessed | tf_op | source)
XLA Modules:
  0.0 359.0 jit_solution(18368750281423588873)
XLA Ops:
  7.2 0.0 copy-start
  7.2 0.0 copy-start.4
  7.2 0.0 all-gather.4.cloned.1.call-start
  7.2 0.7 all-gather.4.cloned.1.call-update
  7.9 0.0 all-gather.6.cloned.1.call-start
  8.0 0.7 all-gather.6.cloned.1.call-update
  8.7 0.9 copy.28
  9.5 1.8 stack.2
  11.4 16.5 %all-to-all-start = ((bf16[64,128,128]{1,2,0:T(8,128)(2,1)}), bf16[64,128,128]{1,2,0:T(8,128)(2,1)S(1)}, u32[]{:S(2)}, u32[]{:S(2)}) async-start(bf16[64,128,128]{1,2,0:T(8,128)(2,1)} %stack.2), calls=%async_computation | async-start | bytes 4194304 | tf_op jit(solution)/shard_map/all_to_all | solution.py:30
  27.9 1.1 copy.26
  28.9 0.8 select_reduce_fusion.1
  29.8 0.0 copy-done
  29.8 1.7 gather_fusion
  31.5 124.5 %all-gather = s32[64,1,128]{2,1,0:T(1,128)S(1)} all-gather(s32[1,1,128]{2,1,0:T(1,128)} %bitcast.74), channel_id=1, replica_groups=mesh['seq'=64,'head'=8] {'seq'}, dimensions={0}, use_global_device_ids=true | all-gather | bytes 33280 | tf_op jit(solution)/shard_map/all_gather | solution.py:32
  156.0 2.4 select_bitcast_fusion
  158.5 0.0 copy-done.4
  158.5 4.4 %fusion.7 = pred[128,8192]{0,1:T(8,128)(4,1)} fusion(s32[128]{0:T(128)S(1)} %iota_add_fusion, s32[128]{0:T(128)S(1)} %copy-done.4, s32[8192]{0:T(1024)S(1)} %bitcast.73), kind=kLoop, calls=%fused_computation.11 | loop fusion | flops 3145728 | bytes 1082368 | tf_op jit(solution)/shard_map/and | solution.py:36
  162.9 0.0 all-to-all-done
  162.9 15.3 %all-to-all-start.1 = ((bf16[2,2,64,16,128]{4,3,1,0,2:T(8,128)(2,1)}), bf16[2,2,64,16,128]{4,3,1,0,2:T(8,128)(2,1)}, u32[]{:S(2)}, u32[]{:S(2)}) async-start(bf16[2,2,64,16,128]{4,3,1,0,2:T(8,128)(2,1)} %select_bitcast_fusion), calls=%async_computation.1 | async-start | bytes 2097152 | tf_op jit(solution)/shard_map/all_to_all | solution.py:91
  178.2 0.2 all-reduce.2.cloned.1.call-start
  178.4 2.7 copy.29
  181.1 2.8 reshape.213
  183.9 0.0 all-gather.4.cloned.1.call-done
  183.9 0.0 copy-start.2
  184.0 5.0 %fusion = (f32[5,128]{1,0:T(8,128)S(1)}, f32[8192,128,5]{1,0,2:T(8,128)S(1)}) fusion(pred[128,8192]{0,1:T(8,128)(4,1)} %fusion.7, bf16[128,5,128]{0,2,1:T(8,128)(2,1)S(1)} %bitcast.71, bf16[8192,128]{1,0:T(8,128)(2,1)} %all-gather.4.cloned.1.call-done), kind=kOutput, calls=%fused_computation.3 | convolution fusion | flops 1357905280 | bytes 24283648 | tf_op jit(solution)/shard_map/tkgd,pkd->kgtp/dot_general | solution.py:44
  189.0 0.0 copy-start.1
  189.0 6.9 %copy-done.1 = f32[8192,128,5]{1,0,2:T(8,128)} copy-done((f32[8192,128,5]{1,0,2:T(8,128)}, f32[8192,128,5]{1,0,2:T(8,128)S(1)}, u32[]{:S(2)}) %copy-start.1) | copy-done | bytes 20971544
  195.9 0.0 copy-done.2
  195.9 5.2 %fusion.1 = f32[5,128]{1,0:T(8,128)S(1)} fusion(f32[8192,128,5]{1,0,2:T(8,128)S(1)} %get-tuple-element.7, f32[5,128]{1,0:T(8,128)S(1)} %broadcast_maximum_fusion, pred[128,8192]{0,1:T(8,128)(4,1)S(1)} %copy-done.2), kind=kLoop, calls=%fused_computation.4 | loop fusion | flops 26213760 | bytes 22025216 | tf_op jit(solution)/shard_map/reduce_sum | solution.py:50
  201.1 9.7 %fusion.13 = bf16[5,128,128]{1,2,0:T(8,128)(2,1)S(1)} fusion(bf16[8192,128,1]{0,1,2:T(8,128)(2,1)S(1)} %reshape.213, f32[8192,128,5]{1,0,2:T(8,128)} %copy-done.1, f32[5,128]{1,0:T(8,128)S(1)} %broadcast_maximum_fusion, pred[128,8192]{0,1:T(8,128)(4,1)S(1)} %copy-done.2, f32[5,128]{1,0:T(8,128)S(1)} %fusion.1), kind=kOutput, calls=%fused_computation.17 | convolution fusion | flops 1368555520 | bytes 24286208 | tf_op jit(solution)/shard_map/kgtp,pkd->kgtd/dot_general | solution.py:51
  210.8 0.0 copy-start.3
  210.9 42.3 %all-gather.6.cloned.1.call-done = bf16[640,5120]{0,1:T(8,128)(2,1)} async-done(((bf16[640,80]{0,1:T(8,128)(2,1)}), bf16[640,5120]{0,1:T(8,128)(2,1)}) %all-gather.6.cloned.1.call-update) | async-done | bytes 6553616 | tf_op jit(solution)/shard_map/all_gather | solution.py:64
  253.1 6.2 %convolution_convert_fusion = bf16[128,5120]{1,0:T(8,128)(2,1)} fusion(bf16[128,640]{0,1:T(8,128)(2,1)S(1)} %bitcast.72, bf16[640,5120]{0,1:T(8,128)(2,1)} %all-gather.6.cloned.1.call-done), kind=kOutput, calls=%fused_computation.9 | convolution fusion | flops 839516160 | bytes 8028160 | tf_op jit(solution)/shard_map/dot_general | solution.py:62
  259.3 0.0 all-reduce.2.cloned.1.call-update
  259.3 0.6 dynamic_slice.14
  259.9 0.6 dynamic_slice.15
  261.8 0.7 iota_compare_fusion.3
  262.5 0.0 all-to-all-done.1
  262.5 2.7 bitcast_select_fusion.1
  265.2 85.6 %all-reduce.2.cloned.1.call-done = bf16[128,5120]{1,0:T(8,128)(2,1)} async-done(((bf16[128,5120]{1,0:T(8,128)(2,1)}), bf16[128,5120]{1,0:T(8,128)(2,1)}) %all-reduce.2.cloned.1.call-update) | async-done | bytes 1310736 | tf_op jit(solution)/shard_map/psum | solution.py:68
  350.8 0.0 copy-done.3
  350.8 1.6 add_convert_fusion
  (5 shorter events, 0.1 us)
Async XLA Ops:
  7.2 22.6 %copy-start = (bf16[2,2,32,16,128]{4,3,2,1,0:T(8,128)(2,1)S(1)}, bf16[2,2,32,16,128]{4,3,2,1,0:T(8,128)(2,1)}, u32[]{:S(2)}) copy-start(bf16[2,2,32,16,128]{4,3,2,1,0:T(8,128)(2,1)} %param.15) | copy-start | bytes 1572868
  7.2 151.3 %copy-start.4 = (s32[128]{0:T(128)S(1)}, s32[128]{0:T(128)}, u32[]{:S(2)}) copy-start(s32[128]{0:T(128)} %param.12) | copy-start | bytes 1540
  7.2 176.7 %all-gather.4.cloned.1.call-start = ((), (), s32[]{:S(2)}) async-start(), calls=%async_computation.2 | async-start | bytes 2129920 | tf_op jit(solution)/shard_map/all_gather | solution.py:28
  7.9 245.2 %all-gather.6.cloned.1.call-start = ((), (), s32[]{:S(2)}) async-start(), calls=%async_computation.3 | async-start | bytes 6656000 | tf_op jit(solution)/shard_map/all_gather | solution.py:64
  11.4 151.5 %all-to-all-start = ((bf16[64,128,128]{1,2,0:T(8,128)(2,1)}), bf16[64,128,128]{1,2,0:T(8,128)(2,1)S(1)}, u32[]{:S(2)}, u32[]{:S(2)}) async-start(bf16[64,128,128]{1,2,0:T(8,128)(2,1)} %stack.2), calls=%async_computation | async-start | bytes 4194304 | tf_op jit(solution)/shard_map/all_to_all | solution.py:30
  162.9 99.6 %all-to-all-start.1 = ((bf16[2,2,64,16,128]{4,3,1,0,2:T(8,128)(2,1)}), bf16[2,2,64,16,128]{4,3,1,0,2:T(8,128)(2,1)}, u32[]{:S(2)}, u32[]{:S(2)}) async-start(bf16[2,2,64,16,128]{4,3,1,0,2:T(8,128)(2,1)} %select_bitcast_fusion), calls=%async_computation.1 | async-start | bytes 2097152 | tf_op jit(solution)/shard_map/all_to_all | solution.py:91
  178.2 172.6 %all-reduce.2.cloned.1.call-start = ((), (), s32[]{:S(2)}) async-start(), calls=%async_computation.4 | async-start | bytes 2621440 | tf_op jit(solution)/shard_map/psum | solution.py:68
  183.9 12.0 %copy-start.2 = (pred[128,8192]{0,1:T(8,128)(4,1)S(1)}, pred[128,8192]{0,1:T(8,128)(4,1)}, u32[]{:S(2)}) copy-start(pred[128,8192]{0,1:T(8,128)(4,1)} %fusion.7) | copy-start | bytes 3145732
  189.0 7.0 %copy-start.1 = (f32[8192,128,5]{1,0,2:T(8,128)}, f32[8192,128,5]{1,0,2:T(8,128)S(1)}, u32[]{:S(2)}) copy-start(f32[8192,128,5]{1,0,2:T(8,128)S(1)} %get-tuple-element.7) | copy-start | bytes 62914564
  210.8 140.0 %copy-start.3 = (bf16[128,640]{1,0:T(8,128)(2,1)S(1)}, bf16[128,640]{1,0:T(8,128)(2,1)}, u32[]{:S(2)}) copy-start(bf16[128,640]{1,0:T(8,128)(2,1)} %param.13) | copy-start | bytes 491524
Sparse Core Ops, SparseCore 0:
  11.3 122.2 all-gather.3
  136.9 116.1 all-gather.5
  259.4 91.3 all-reduce.1
